TPU v7x, 32 devices: a whole 2x2x4 slice. The times are simulated.
32 devices in a mesh: layer: 8 (over z, x), batch: 4 (over y, core).
Axes of the slice: x: 2, y: 2, z: 4, core: 2. Of those that a mesh axis runs over, the one named last changes fastest.
Arguments:
- inputs: float32 [4, 8, 8, 8, 128], P('batch'), parts along dimension 0, may hold values from -6 to 6
- guess_states: float32 [32, 4, 8, 8, 8, 128], P('layer', 'batch'), parts along dimension 1, may hold values from -6 to 6
- kernels: bfloat16 [32, 3, 3, 3, 128, 128], P('layer'), may hold values from -0.109375 to 0.109375
- biases: float32 [32, 128], P('layer'), may hold values from -4 to 4
Outputs:
- states: float32 [32, 4, 8, 8, 8, 128], P('layer', 'batch'), parts along dimension 1
- coarse_residual: float32 [8, 4, 8, 8, 8, 128], P('layer', 'batch'), parts along dimension 1
There are 4 independent parts, one for each index of `batch`. A program takes and returns all parts, laid end to end along the dimension named above; an argument that names none is the same for every part. Nothing has to cross between parts.
All inputs are finite; a program needn't handle non-finite values.
Results may differ from a plain program's by a relative error of at most 0.0008.
Values may be sent and summed in bfloat16 or wider, within the bound.
A program may use at most 128 MiB of HBM per device.

v0:
```python
import jax
import jax.numpy as jnp
from jax import lax
from jax.experimental import pallas as pl
from jax.experimental.pallas import tpu as pltpu
from jax.sharding import PartitionSpec as P

COARSEN = 4
TAPS = 3
MESH = pl.DeviceIdType.MESH


def cycle_kernel(sections, inputs_ref, guess_ref, kern_ref, bias_ref, states_ref, residual_ref,
                 fine_w, lead_w, patches, cur, head, head_mix, first_head, next_head, corner_out,
                 start_in, group_in, top_head, top_rhs, defects, top_in, top_out,
                 load_sem, lead_sem, hop_send, hop_recv, w_send, w_recv, sib_send, sib_recv,
                 head_send, head_recv, g_send, g_recv, jump_send, jump_recv):
    depth = guess_ref.shape[0]
    size_x, size_y, size_z, width = inputs_ref.shape
    groups = sections // COARSEN
    fine_size = 2.0 / (depth * sections)
    coarse_size = depth * fine_size
    top_size = COARSEN * coarse_size
    rows = TAPS * TAPS * width
    half_rows = rows // 2
    me = lax.axis_index("layer")
    part = lax.axis_index("batch")
    pos = lax.rem(me, COARSEN)
    group = me // COARSEN
    core = lax.rem(part, 2)
    sibling = part + 1 - 2 * core
    is_first = me == 0
    has_next = me < sections - 1
    has_group_before = group > 0
    has_group_after = group < groups - 1

    def peer(rel):
        return (group * COARSEN + lax.rem(pos + rel, COARSEN), part)

    def slot_from(rel):
        return lax.rem(pos + COARSEN - rel, COARSEN)

    def fine_load(layer, tap):
        return pltpu.make_async_copy(
            kern_ref.at[layer, tap],
            fine_w.at[layer, :, pl.ds(tap * width, width)],
            load_sem.at[layer, tap],
        )

    def lead_load(tap):
        return pltpu.make_async_copy(
            kern_ref.at[0, tap],
            lead_w.at[pos, :, pl.ds(tap * width, width)],
            lead_sem.at[tap],
        )

    for layer in range(depth):
        for tap in range(TAPS):
            fine_load(layer, tap).start()
    for tap in range(TAPS):
        lead_load(tap).start()

    barrier = pltpu.get_barrier_semaphore()

    def greet(device):
        pl.semaphore_signal(barrier, inc=1, device_id=device, device_id_type=MESH)

    partners = [(has_next, (me + 1, part)), (me > 0, (me - 1, part)),
                (has_group_after, (me + COARSEN, part)), (has_group_before, (me - COARSEN, part))]
    for there, device in partners:
        pl.when(there)(lambda device=device: greet(device))
    for rel in range(1, COARSEN):
        greet(peer(rel))
    greet((me, sibling))
    greetings = sum(jnp.where(there, 1, 0) for there, _ in partners)
    pl.semaphore_wait(barrier, COARSEN + greetings)

    def hop(index, source, target):
        return pltpu.make_async_remote_copy(
            src_ref=source, dst_ref=target, send_sem=hop_send.at[index], recv_sem=hop_recv.at[index],
            device_id=(me + 1, part), device_id_type=MESH)

    first_hop = hop(0, guess_ref.at[depth - 1, 0], first_head)
    second_hop = hop(1, corner_out, next_head)
    pl.when(has_next)(first_hop.start)

    def half(which):
        return pl.ds(pl.multiple_of(which * half_rows, 16), half_rows)

    def w_copy(rel):
        return pltpu.make_async_remote_copy(
            src_ref=lead_w.at[pos, half(core)], dst_ref=lead_w.at[pos, half(core)],
            send_sem=w_send.at[rel], recv_sem=w_recv.at[rel],
            device_id=peer(rel), device_id_type=MESH)

    def w_arrival(rel):
        return pltpu.make_async_remote_copy(
            src_ref=lead_w.at[slot_from(rel), half(core)], dst_ref=lead_w.at[slot_from(rel), half(core)],
            send_sem=w_send.at[rel], recv_sem=w_recv.at[rel],
            device_id=peer(rel), device_id_type=MESH)

    def sib_copy(rel, which):
        return pltpu.make_async_remote_copy(
            src_ref=lead_w.at[slot_from(rel), half(which)], dst_ref=lead_w.at[slot_from(rel), half(which)],
            send_sem=sib_send.at[rel], recv_sem=sib_recv.at[rel],
            device_id=(me, sibling), device_id_type=MESH)

    for tap in range(TAPS):
        lead_load(tap).wait()
    for rel in range(1, COARSEN):
        w_copy(rel).start()

    z_index = lax.broadcasted_iota(jnp.int32, (size_x * size_y, size_z, width), 1)

    def mix(state, weights):
        squashed = jnp.tanh(state).reshape(size_x * size_y, size_z, width)
        below = jnp.where(z_index == 0, 0.0, pltpu.roll(squashed, 1, 1))
        above = jnp.where(z_index == size_z - 1, 0.0, pltpu.roll(squashed, size_z - 1, 1))
        edge = jnp.zeros((size_x, 1, size_z, width), jnp.float32)
        span = size_y * size_z
        for tap_z, shifted in enumerate((below, squashed, above)):
            shifted = shifted.reshape(size_x, size_y, size_z, width)
            even = shifted.reshape(size_x, span, width).astype(jnp.bfloat16)
            odd = jnp.concatenate([edge, shifted, edge], 1)
            odd = odd.reshape(size_x, span + 2 * size_z, width).astype(jnp.bfloat16)
            for tap_y, block in enumerate((odd[:, :span], even, odd[:, 2 * size_z:])):
                column = (tap_y * TAPS + tap_z) * width
                patches[:, :, column:column + width] = block
        left = patches[...].reshape(size_x * span, rows)
        product = jnp.dot(left, weights[...], preferred_element_type=jnp.float32)
        product = product.reshape(size_x, size_y, size_z, TAPS * width)
        plane = jnp.zeros((1, size_y, size_z, width), jnp.float32)
        total = product[..., width:2 * width]
        total = total + jnp.concatenate([plane, product[:-1, :, :, :width]], 0)
        return total + jnp.concatenate([product[1:, :, :, 2 * width:], plane], 0)

    def fine_step(layer):
        state = cur[...]
        mixed = mix(state, fine_w.at[layer])
        return state, mixed, state + fine_size * (mixed + bias_ref[layer])

    pl.when(has_next)(first_hop.wait_send)
    pl.when(me > 0)(first_hop.wait_recv)
    cur[...] = jnp.where(is_first, inputs_ref[...], first_head[...])

    for layer in range(depth):
        for tap in range(TAPS):
            fine_load(layer, tap).wait()

    def sweep_one(layer, carry):
        cur[...] = fine_step(layer)[2]
        return carry

    lax.fori_loop(0, depth, sweep_one, 0)
    corner_out[...] = cur[...]
    pl.when(has_next)(second_hop.start)

    for rel in range(1, COARSEN):
        w_arrival(rel).wait_recv()
        sib_copy(rel, core).start()

    pl.when(has_next)(second_hop.wait_send)
    pl.when(me > 0)(second_hop.wait_recv)

    def head_copy(rel):
        return pltpu.make_async_remote_copy(
            src_ref=next_head, dst_ref=group_in, send_sem=head_send.at[rel], recv_sem=head_recv,
            device_id=peer(rel), device_id_type=MESH)

    leads_group = jnp.logical_and(pos == 0, has_group_before)
    follows = jnp.logical_and(pos > 0, has_group_before)
    for rel in range(1, COARSEN):
        pl.when(leads_group)(head_copy(rel).start)
    head[...] = jnp.where(is_first, inputs_ref[...], next_head[...])
    cur[...] = head[...]

    def sweep_two(layer, carry):
        _, mixed, after = fine_step(layer)

        @pl.when(layer == 0)
        def _():
            head_mix[...] = mixed

        cur[...] = after
        return carry

    lax.fori_loop(0, depth, sweep_two, 0)
    defects[pos] = cur[...] - head[...] - coarse_size * head_mix[...]

    def g_copy(rel):
        return pltpu.make_async_remote_copy(
            src_ref=defects.at[pos], dst_ref=defects.at[pos],
            send_sem=g_send.at[rel], recv_sem=g_recv.at[rel], device_id=peer(rel), device_id_type=MESH)

    def g_arrival(rel):
        return pltpu.make_async_remote_copy(
            src_ref=defects.at[slot_from(rel)], dst_ref=defects.at[slot_from(rel)],
            send_sem=g_send.at[rel], recv_sem=g_recv.at[rel], device_id=peer(rel), device_id_type=MESH)

    for rel in range(1, COARSEN):
        g_copy(rel).start()

    pl.when(follows)(head_copy(1).wait_recv)

    @pl.when(group == 0)
    def _():
        cur[...] = inputs_ref[...]

    @pl.when(leads_group)
    def _():
        cur[...] = next_head[...]

    @pl.when(follows)
    def _():
        cur[...] = group_in[...]

    for rel in range(1, COARSEN):
        sib_copy(rel, 1 - core).wait_recv()
        g_arrival(rel).wait_recv()

    def chain(count):
        def step(turn, carry):
            state = cur[...]
            mixed = mix(state, lead_w.at[turn])

            @pl.when(turn == pos)
            def _():
                head[...] = state
                head_mix[...] = mixed

            after = state + coarse_size * mixed + defects[turn]
            cur[...] = after
            return carry

        lax.fori_loop(0, COARSEN, step, 0)

    def jump(index, source, target):
        return pltpu.make_async_remote_copy(
            src_ref=source, dst_ref=target, send_sem=jump_send.at[index], recv_sem=jump_recv.at[index],
            device_id=(me + COARSEN, part), device_id_type=MESH)

    chain(COARSEN)
    corner_out[...] = cur[...]
    relaxed = jump(0, corner_out, start_in)
    pl.when(has_group_after)(relaxed.start)
    pl.when(has_group_after)(relaxed.wait_send)
    pl.when(has_group_before)(relaxed.wait_recv)
    group_in_first = group == 0

    def started():
        return jnp.where(group_in_first, inputs_ref[...], start_in[...])

    cur[...] = started()
    chain(COARSEN)
    is_owner = pos == COARSEN - 1
    corner = cur[...]
    residual_ref[0, 0] = jnp.where(is_owner, corner - corner_out[...], corner - corner)

    top_w = lead_w.at[COARSEN - 1]
    top_rhs[...] = corner - started() - top_size * mix(started(), top_w)
    solved = jump(1, top_out, top_in)
    pl.when(has_group_before)(solved.wait_recv)
    top_head[...] = jnp.where(group_in_first, inputs_ref[...], top_in[...])
    top_out[...] = top_head[...] + top_size * mix(top_head[...], top_w) + top_rhs[...]
    pl.when(has_group_after)(solved.start)

    cur[...] = top_head[...]
    chain(COARSEN)

    first = head[...] + coarse_size * head_mix[...] + defects[pos]
    states_ref[depth - 1, 0] = jnp.where(is_owner, top_out[...], first)
    cur[...] = head[...] + fine_size * (head_mix[...] + bias_ref[0])
    states_ref[0, 0] = cur[...]

    def last_sweep(layer, carry):
        after = fine_step(layer)[2]
        cur[...] = after
        states_ref[layer, 0] = after
        return carry

    lax.fori_loop(1, depth - 1, last_sweep, 0)

    for rel in range(1, COARSEN):
        w_copy(rel).wait_send()
        sib_copy(rel, core).wait_send()
        g_copy(rel).wait_send()
        pl.when(leads_group)(head_copy(rel).wait_send)
    pl.when(has_group_after)(solved.wait_send)


def shards(inputs, guess_states, kernels, biases):
    sections = lax.axis_size("layer")
    depth = guess_states.shape[0]
    state = inputs.shape[1:]
    width = state[-1]
    rows = TAPS * TAPS * width
    vmem = pl.BlockSpec(memory_space=pltpu.VMEM)
    anywhere = pl.BlockSpec(memory_space=pl.ANY)
    kernel_rows = kernels.reshape(depth, TAPS, rows, width)
    bias_rows = biases.reshape(depth, 1, 1, width)
    f32_state = pltpu.VMEM(state, jnp.float32)
    dma = pltpu.SemaphoreType.DMA

    def body(*refs):
        cycle_kernel(sections, *refs)

    return tuple(pl.pallas_call(
        body,
        name="mgrit_cycle",
        out_shape=(
            jax.ShapeDtypeStruct(guess_states.shape, jnp.float32),
            jax.ShapeDtypeStruct((1,) + guess_states.shape[1:], jnp.float32),
        ),
        in_specs=[vmem, anywhere, anywhere, vmem],
        out_specs=(vmem, vmem),
        scratch_shapes=[
            pltpu.VMEM((depth, rows, TAPS * width), jnp.bfloat16),
            pltpu.VMEM((COARSEN, rows, TAPS * width), jnp.bfloat16),
            pltpu.VMEM((state[0], state[1] * state[2], rows), jnp.bfloat16),
            f32_state, f32_state, f32_state, f32_state, f32_state, f32_state,
            f32_state, f32_state, f32_state, f32_state,
            pltpu.VMEM((COARSEN,) + state, jnp.float32),
            f32_state, f32_state,
            dma((depth, TAPS)), dma((TAPS,)), dma((2,)), dma((2,)),
            dma((COARSEN,)), dma((COARSEN,)), dma((COARSEN,)), dma((COARSEN,)),
            dma((COARSEN,)), dma, dma((COARSEN,)), dma((COARSEN,)), dma((2,)), dma((2,)),
        ],
        compiler_params=pltpu.CompilerParams(
            collective_id=0, has_side_effects=True, vmem_limit_bytes=48 * 1024 * 1024),
    )(inputs.reshape(state), guess_states, kernel_rows, bias_rows))


def solution(mesh):
    return jax.shard_map(
        shards,
        mesh=mesh,
        in_specs=(
            P("batch", None, None, None, None),
            P("layer", "batch", None, None, None, None),
            P("layer", None, None, None, None, None),
            P("layer", None),
        ),
        out_specs=(
            P("layer", "batch", None, None, None, None),
            P("layer", "batch", None, None, None, None),
        ),
        check_vma=False,
    )
```

profile of v0, /device:TPU:24, one launch (start us, length us, event | category | flops | bytes accessed | tf_op | source)
XLA Modules:
  0.0 96.3 jit_solution(15225378996070003191)
XLA Ops:
  0.6 0.0 copy-start
  0.6 2.0 %copy-done = bf16[4,3,3,3,128,128]{5,4,3,2,1,0:T(8,128)(2,1)S(1)} copy-done((bf16[4,3,3,3,128,128]{5,4,3,2,1,0:T(8,128)(2,1)S(1)}, bf16[4,3,3,3,128,128]{5,4,3,2,1,0:T(8,128)(2,1)}, u32[]{:S(2)}) %copy-start) | copy-done | bytes 3538968
  2.6 0.0 copy-start.1
  2.6 1.2 %copy-done.1 = f32[4,1,8,8,8,128]{5,4,3,2,1,0:T(8,128)S(1)} copy-done((f32[4,1,8,8,8,128]{5,4,3,2,1,0:T(8,128)S(1)}, f32[4,1,8,8,8,128]{5,4,3,2,1,0:T(8,128)}, u32[]{:S(2)}) %copy-start.1) | copy-done | bytes 1048600
  3.9 0.0 copy-start.2
  3.9 0.9 copy-done.2
  4.8 0.0 copy-start.3
  4.8 0.7 copy-done.3
  5.5 89.1 %mgrit_cycle.1 = (f32[4,1,8,8,8,128]{5,4,3,2,1,0:T(8,128)S(1)}, f32[1,1,8,8,8,128]{5,4,3,2,1,0:T(8,128)S(1)}) custom-call(f32[8,8,8,128]{3,2,1,0:T(8,128)S(1)} %bitcast.4, f32[4,1,8,8,8,128]{5,4,3,2,1,0:T(8,128)S(1)} %copy-done.1, bf16[4,3,1152,128]{3,2,1,0:T(8,128)(2,1)S(1)} %bitcast.3, f32[4,1,1,128]{3,2,1,0:T(1,128)S(1)} %bitcast.5), custom_call_target="tpu_custom_call" | custom-call | tf_op jit(solution)/shard_map/mgrit_cycle/pallas_call | solution.py:307
  94.6 1.0 %copy.8 = f32[4,1,8,8,8,128]{5,4,3,2,1,0:T(8,128)} copy(f32[4,1,8,8,8,128]{5,4,3,2,1,0:T(8,128)S(1)} %get-tuple-element.4) | data formatting | bytes 2097152
  95.6 0.7 copy.9
Async XLA Ops:
  0.6 2.0 %copy-start = (bf16[4,3,3,3,128,128]{5,4,3,2,1,0:T(8,128)(2,1)S(1)}, bf16[4,3,3,3,128,128]{5,4,3,2,1,0:T(8,128)(2,1)}, u32[]{:S(2)}) copy-start(bf16[4,3,3,3,128,128]{5,4,3,2,1,0:T(8,128)(2,1)} %param.6) | copy-start | bytes 10616836
  2.6 1.2 %copy-start.1 = (f32[4,1,8,8,8,128]{5,4,3,2,1,0:T(8,128)S(1)}, f32[4,1,8,8,8,128]{5,4,3,2,1,0:T(8,128)}, u32[]{:S(2)}) copy-start(f32[4,1,8,8,8,128]{5,4,3,2,1,0:T(8,128)} %refs_1_.1) | copy-start | bytes 3145732
  3.9 0.9 copy-start.2
  4.8 0.7 copy-start.3
where the time goes:
time: 96.6 us; the launch traced here: 96.3 us
  Pallas kernels  89.1 us (92%)
  local copies, waits for them, and re-layouts  6.52 us (7%)
    pallas_call x1, Pallas kernels, shards(): pl.pallas_call(body, name='mgrit_cycle', out_shape=(jax.ShapeDtypeStruct(...  89.1 us
    unnamed x10, local copies, waits for them, and re-layouts  6.52 us

commit v1 on v0

--- a/solution.py
+++ b/solution.py
@@ -33,9 +33,20 @@
     has_next = me < sections - 1
     has_group_before = group > 0
     has_group_after = group < groups - 1
+    span_low = COARSEN // 2
+    is_upper = pos >= span_low
 
     def peer(rel):
         return (group * COARSEN + lax.rem(pos + rel, COARSEN), part)
+
+    def wanted(source, target):
+        return jnp.logical_or(target >= span_low, target > source)
+
+    def gives(rel):
+        return wanted(pos, lax.rem(pos + rel, COARSEN))
+
+    def takes(rel):
+        return wanted(slot_from(rel), pos)
 
     def slot_from(rel):
         return lax.rem(pos + COARSEN - rel, COARSEN)
@@ -66,7 +77,9 @@
         pl.semaphore_signal(barrier, inc=1, device_id=device, device_id_type=MESH)
 
     partners = [(has_next, (me + 1, part)), (me > 0, (me - 1, part)),
-                (has_group_after, (me + COARSEN, part)), (has_group_before, (me - COARSEN, part))]
+                (has_group_after, (me + COARSEN, part)), (has_group_before, (me - COARSEN, part)),
+                (jnp.logical_and(is_upper, has_group_after), (me + COARSEN - span_low, part)),
+                (jnp.logical_and(pos < span_low, has_group_before), (me - COARSEN + span_low, part))]
     for there, device in partners:
         pl.when(there)(lambda device=device: greet(device))
     for rel in range(1, COARSEN):
@@ -107,8 +120,9 @@
 
     for tap in range(TAPS):
         lead_load(tap).wait()
-    for rel in range(1, COARSEN):
-        w_copy(rel).start()
+    early = (None, pos != 1, pos >= 0, pos == COARSEN - 1)
+    for rel in (1, 2, 3):
+        pl.when(jnp.logical_and(gives(rel), early[rel]))(w_copy(rel).start)
 
     z_index = lax.broadcasted_iota(jnp.int32, (size_x * size_y, size_z, width), 1)
 
@@ -155,9 +169,8 @@
     corner_out[...] = cur[...]
     pl.when(has_next)(second_hop.start)
 
-    for rel in range(1, COARSEN):
-        w_arrival(rel).wait_recv()
-        sib_copy(rel, core).start()
+    for rel in (1, 2, 3):
+        pl.when(jnp.logical_and(gives(rel), jnp.logical_not(early[rel])))(w_copy(rel).start)
 
     pl.when(has_next)(second_hop.wait_send)
     pl.when(me > 0)(second_hop.wait_recv)
@@ -168,9 +181,7 @@
             device_id=peer(rel), device_id_type=MESH)
 
     leads_group = jnp.logical_and(pos == 0, has_group_before)
-    follows = jnp.logical_and(pos > 0, has_group_before)
-    for rel in range(1, COARSEN):
-        pl.when(leads_group)(head_copy(rel).start)
+    follows = jnp.logical_and(is_upper, has_group_before)
     head[...] = jnp.where(is_first, inputs_ref[...], next_head[...])
     cur[...] = head[...]
 
@@ -197,26 +208,23 @@
             src_ref=defects.at[slot_from(rel)], dst_ref=defects.at[slot_from(rel)],
             send_sem=g_send.at[rel], recv_sem=g_recv.at[rel], device_id=peer(rel), device_id_type=MESH)
 
+    for rel in range(COARSEN - 1, 0, -1):
+        pl.when(gives(rel))(g_copy(rel).start)
+    for rel in range(span_low, COARSEN):
+        pl.when(leads_group)(head_copy(rel).start)
     for rel in range(1, COARSEN):
-        g_copy(rel).start()
-
+        @pl.when(takes(rel))
+        def _(rel=rel):
+            w_arrival(rel).wait_recv()
+            sib_copy(rel, core).start()
+
+    group_in_first = group == 0
     pl.when(follows)(head_copy(1).wait_recv)
-
-    @pl.when(group == 0)
-    def _():
-        cur[...] = inputs_ref[...]
-
-    @pl.when(leads_group)
-    def _():
-        cur[...] = next_head[...]
-
-    @pl.when(follows)
-    def _():
-        cur[...] = group_in[...]
-
     for rel in range(1, COARSEN):
-        sib_copy(rel, 1 - core).wait_recv()
-        g_arrival(rel).wait_recv()
+        @pl.when(takes(rel))
+        def _(rel=rel):
+            sib_copy(rel, 1 - core).wait_recv()
+            g_arrival(rel).wait_recv()
 
     def chain(count):
         def step(turn, carry):
@@ -232,40 +240,55 @@
             cur[...] = after
             return carry
 
-        lax.fori_loop(0, COARSEN, step, 0)
-
-    def jump(index, source, target):
-        return pltpu.make_async_remote_copy(
-            src_ref=source, dst_ref=target, send_sem=jump_send.at[index], recv_sem=jump_recv.at[index],
-            device_id=(me + COARSEN, part), device_id_type=MESH)
-
-    chain(COARSEN)
-    corner_out[...] = cur[...]
-    relaxed = jump(0, corner_out, start_in)
-    pl.when(has_group_after)(relaxed.start)
-    pl.when(has_group_after)(relaxed.wait_send)
-    pl.when(has_group_before)(relaxed.wait_recv)
-    group_in_first = group == 0
-
-    def started():
-        return jnp.where(group_in_first, inputs_ref[...], start_in[...])
-
-    cur[...] = started()
-    chain(COARSEN)
+        lax.fori_loop(0, count, step, 0)
+
+    def jump(index, source, target, back):
+        return pltpu.make_async_remote_copy(
+            src_ref=source, dst_ref=target, send_sem=jump_send.at[index], recv_sem=jump_recv.at[min(index, 1)],
+            device_id=(me + COARSEN - back, part), device_id_type=MESH)
+
+    relaxed = jump(0, corner_out, start_in, 0)
+    solved = jump(1, top_out, top_in, 0)
+    solved_low = jump(2, top_out, top_in, span_low)
+    upper_sends = jnp.logical_and(is_upper, has_group_after)
     is_owner = pos == COARSEN - 1
-    corner = cur[...]
-    residual_ref[0, 0] = jnp.where(is_owner, corner - corner_out[...], corner - corner)
-
-    top_w = lead_w.at[COARSEN - 1]
-    top_rhs[...] = corner - started() - top_size * mix(started(), top_w)
-    solved = jump(1, top_out, top_in)
-    pl.when(has_group_before)(solved.wait_recv)
-    top_head[...] = jnp.where(group_in_first, inputs_ref[...], top_in[...])
-    top_out[...] = top_head[...] + top_size * mix(top_head[...], top_w) + top_rhs[...]
-    pl.when(has_group_after)(solved.start)
+
+    @pl.when(is_upper)
+    def _():
+        cur[...] = jnp.where(group_in_first, inputs_ref[...], group_in[...])
+        chain(COARSEN)
+        corner_out[...] = cur[...]
+        pl.when(upper_sends)(relaxed.start)
+        pl.when(follows)(relaxed.wait_recv)
+        start = jnp.where(group_in_first, inputs_ref[...], start_in[...])
+        top_head[...] = start
+        cur[...] = start
+        chain(COARSEN)
+        top_w = lead_w.at[COARSEN - 1]
+        start = top_head[...]
+        top_rhs[...] = cur[...] - start - top_size * mix(start, top_w)
+        corner = cur[...]
+        residual_ref[0, 0] = jnp.where(is_owner, corner - corner_out[...], corner - corner)
+        pl.when(follows)(solved.wait_recv)
+        top_head[...] = jnp.where(group_in_first, inputs_ref[...], top_in[...])
+        top_out[...] = top_head[...] + top_size * mix(top_head[...], top_w) + top_rhs[...]
+        pl.when(upper_sends)(solved.start)
+        pl.when(upper_sends)(solved_low.start)
+
+    lower_takes = jnp.logical_and(pos < span_low, has_group_before)
+    pl.when(lower_takes)(solved_low.wait_recv)
+
+    @pl.when(pos < span_low)
+    def _():
+        top_head[...] = jnp.where(group_in_first, inputs_ref[...], top_in[...])
 
     cur[...] = top_head[...]
-    chain(COARSEN)
+    chain(pos + 1)
+
+    @pl.when(pos < span_low)
+    def _():
+        corner = cur[...]
+        residual_ref[0, 0] = corner - corner
 
     first = head[...] + coarse_size * head_mix[...] + defects[pos]
     states_ref[depth - 1, 0] = jnp.where(is_owner, top_out[...], first)
@@ -281,11 +304,13 @@
     lax.fori_loop(1, depth - 1, last_sweep, 0)
 
     for rel in range(1, COARSEN):
-        w_copy(rel).wait_send()
-        sib_copy(rel, core).wait_send()
-        g_copy(rel).wait_send()
+        pl.when(gives(rel))(w_copy(rel).wait_send)
+        pl.when(takes(rel))(sib_copy(rel, core).wait_send)
+        pl.when(gives(rel))(g_copy(rel).wait_send)
+    for rel in range(span_low, COARSEN):
         pl.when(leads_group)(head_copy(rel).wait_send)
-    pl.when(has_group_after)(solved.wait_send)
+    for copy in (relaxed, solved, solved_low):
+        pl.when(upper_sends)(copy.wait_send)
 
 
 def shards(inputs, guess_states, kernels, biases):
@@ -323,10 +348,10 @@
             f32_state, f32_state,
             dma((depth, TAPS)), dma((TAPS,)), dma((2,)), dma((2,)),
             dma((COARSEN,)), dma((COARSEN,)), dma((COARSEN,)), dma((COARSEN,)),
-            dma((COARSEN,)), dma, dma((COARSEN,)), dma((COARSEN,)), dma((2,)), dma((2,)),
+            dma((COARSEN,)), dma, dma((COARSEN,)), dma((COARSEN,)), dma((3,)), dma((2,)),
         ],
         compiler_params=pltpu.CompilerParams(
-            collective_id=0, has_side_effects=True, vmem_limit_bytes=48 * 1024 * 1024),
+            collective_id=0, has_side_effects=True, vmem_limit_bytes=60 * 1024 * 1024),
     )(inputs.reshape(state), guess_states, kernel_rows, bias_rows))
 
 

time: 96.6 us -> 83.6 us (0.87)
  the two profiles are of different devices: /device:TPU:24 before, /device:TPU:16 now
where the time goes in v1:
time: 83.6 us; the launch traced here: 83.4 us
  Pallas kernels  78.7 us (94%)
  local copies, waits for them, and re-layouts  3.98 us (5%)
    pallas_call x1, Pallas kernels, shards(): pl.pallas_call(body, name='mgrit_cycle', out_shape=(jax.ShapeDtypeStruct(...  78.7 us
    unnamed x2, local copies, waits for them, and re-layouts  3.98 us

profile of v1, /device:TPU:16, one launch (start us, length us, event | category | flops | bytes accessed | tf_op | source)
XLA Modules:
  0.0 83.4 jit_solution(12958195027387861517)
XLA Ops:
  0.6 78.7 %mgrit_cycle.1 = (f32[4,1,8,8,8,128]{5,4,3,2,1,0:T(8,128)}, f32[1,1,8,8,8,128]{5,4,3,2,1,0:T(8,128)}) custom-call(f32[8,8,8,128]{3,2,1,0:T(8,128)} %bitcast.4, f32[4,1,8,8,8,128]{5,4,3,2,1,0:T(8,128)} %refs_1_.1, bf16[4,3,1152,128]{3,2,1,0:T(8,128)(2,1)} %bitcast.3, f32[4,1,1,128]{3,2,1,0:T(1,128)} %bitcast.5), custom_call_target="tpu_custom_call" | custom-call | tf_op jit(solution)/shard_map/mgrit_cycle/pallas_call | solution.py:332
  79.4 2.3 %copy.8 = f32[4,1,8,8,8,128]{5,4,3,2,1,0:T(8,128)} copy(f32[4,1,8,8,8,128]{5,4,3,2,1,0:T(8,128)} %get-tuple-element.4) | data formatting | bytes 2097152
  81.7 1.7 %copy.9 = f32[1,1,8,8,8,128]{5,4,3,2,1,0:T(8,128)} copy(f32[1,1,8,8,8,128]{5,4,3,2,1,0:T(8,128)} %get-tuple-element.5) | data formatting | bytes 524288

commit v2 on v1

--- a/solution.py
+++ b/solution.py
@@ -10,10 +10,11 @@
 MESH = pl.DeviceIdType.MESH
 
 
-def cycle_kernel(sections, inputs_ref, guess_ref, kern_ref, bias_ref, states_ref, residual_ref,
+def cycle_kernel(sections, inputs_hbm, guess_ref, kern_ref, bias_hbm, states_ref, residual_ref,
+                 inputs_ref, bias_ref,
                  fine_w, lead_w, patches, cur, head, head_mix, first_head, next_head, corner_out,
                  start_in, group_in, top_head, top_rhs, defects, top_in, top_out,
-                 load_sem, lead_sem, hop_send, hop_recv, w_send, w_recv, sib_send, sib_recv,
+                 load_sem, lead_sem, small_sem, hop_send, hop_recv, w_send, w_recv, sib_send, sib_recv,
                  head_send, head_recv, g_send, g_recv, jump_send, jump_recv):
     depth = guess_ref.shape[0]
     size_x, size_y, size_z, width = inputs_ref.shape
@@ -65,11 +66,15 @@
             lead_sem.at[tap],
         )
 
+    inputs_load = pltpu.make_async_copy(inputs_hbm, inputs_ref, small_sem.at[0])
+    bias_load = pltpu.make_async_copy(bias_hbm, bias_ref, small_sem.at[1])
+    for tap in range(TAPS):
+        lead_load(tap).start()
+    inputs_load.start()
+    bias_load.start()
     for layer in range(depth):
         for tap in range(TAPS):
             fine_load(layer, tap).start()
-    for tap in range(TAPS):
-        lead_load(tap).start()
 
     barrier = pltpu.get_barrier_semaphore()
 
@@ -130,13 +135,12 @@
         squashed = jnp.tanh(state).reshape(size_x * size_y, size_z, width)
         below = jnp.where(z_index == 0, 0.0, pltpu.roll(squashed, 1, 1))
         above = jnp.where(z_index == size_z - 1, 0.0, pltpu.roll(squashed, size_z - 1, 1))
-        edge = jnp.zeros((size_x, 1, size_z, width), jnp.float32)
         span = size_y * size_z
+        edge = jnp.zeros((size_x, size_z, width), jnp.float32)
         for tap_z, shifted in enumerate((below, squashed, above)):
-            shifted = shifted.reshape(size_x, size_y, size_z, width)
-            even = shifted.reshape(size_x, span, width).astype(jnp.bfloat16)
-            odd = jnp.concatenate([edge, shifted, edge], 1)
-            odd = odd.reshape(size_x, span + 2 * size_z, width).astype(jnp.bfloat16)
+            shifted = shifted.reshape(size_x, span, width)
+            even = shifted.astype(jnp.bfloat16)
+            odd = jnp.concatenate([edge, shifted, edge], 1).astype(jnp.bfloat16)
             for tap_y, block in enumerate((odd[:, :span], even, odd[:, 2 * size_z:])):
                 column = (tap_y * TAPS + tap_z) * width
                 patches[:, :, column:column + width] = block
@@ -155,6 +159,8 @@
 
     pl.when(has_next)(first_hop.wait_send)
     pl.when(me > 0)(first_hop.wait_recv)
+    inputs_load.wait()
+    bias_load.wait()
     cur[...] = jnp.where(is_first, inputs_ref[...], first_head[...])
 
     for layer in range(depth):
@@ -262,8 +268,12 @@
         pl.when(follows)(relaxed.wait_recv)
         start = jnp.where(group_in_first, inputs_ref[...], start_in[...])
         top_head[...] = start
-        cur[...] = start
-        chain(COARSEN)
+
+        @pl.when(has_group_before)
+        def _():
+            cur[...] = start_in[...]
+            chain(COARSEN)
+
         top_w = lead_w.at[COARSEN - 1]
         start = top_head[...]
         top_rhs[...] = cur[...] - start - top_size * mix(start, top_w)
@@ -320,7 +330,7 @@
     width = state[-1]
     rows = TAPS * TAPS * width
     vmem = pl.BlockSpec(memory_space=pltpu.VMEM)
-    anywhere = pl.BlockSpec(memory_space=pl.ANY)
+    hbm = pl.BlockSpec(memory_space=pltpu.HBM)
     kernel_rows = kernels.reshape(depth, TAPS, rows, width)
     bias_rows = biases.reshape(depth, 1, 1, width)
     f32_state = pltpu.VMEM(state, jnp.float32)
@@ -336,9 +346,10 @@
             jax.ShapeDtypeStruct(guess_states.shape, jnp.float32),
             jax.ShapeDtypeStruct((1,) + guess_states.shape[1:], jnp.float32),
         ),
-        in_specs=[vmem, anywhere, anywhere, vmem],
+        in_specs=[hbm, hbm, hbm, hbm],
         out_specs=(vmem, vmem),
         scratch_shapes=[
+            f32_state, pltpu.VMEM(bias_rows.shape, jnp.float32),
             pltpu.VMEM((depth, rows, TAPS * width), jnp.bfloat16),
             pltpu.VMEM((COARSEN, rows, TAPS * width), jnp.bfloat16),
             pltpu.VMEM((state[0], state[1] * state[2], rows), jnp.bfloat16),
@@ -346,7 +357,7 @@
             f32_state, f32_state, f32_state, f32_state,
             pltpu.VMEM((COARSEN,) + state, jnp.float32),
             f32_state, f32_state,
-            dma((depth, TAPS)), dma((TAPS,)), dma((2,)), dma((2,)),
+            dma((depth, TAPS)), dma((TAPS,)), dma((2,)), dma((2,)), dma((2,)),
             dma((COARSEN,)), dma((COARSEN,)), dma((COARSEN,)), dma((COARSEN,)),
             dma((COARSEN,)), dma, dma((COARSEN,)), dma((COARSEN,)), dma((3,)), dma((2,)),
         ],

time: 83.6 us -> 82.6 us (0.988)
  Pallas kernels: 78.7 us -> 77.8 us
    pallas_call x1, Pallas kernels: 78.7 us -> 77.8 us  [shards(): pl.pallas_call(body, name='mgrit_cycle', out_shape=(jax.ShapeDtypeStruct(...]
where the time goes in v2:
time: 82.6 us; the launch traced here: 82.5 us
  Pallas kernels  77.8 us (94%)
  local copies, waits for them, and re-layouts  3.98 us (5%)
    pallas_call x1, Pallas kernels, shards(): pl.pallas_call(body, name='mgrit_cycle', out_shape=(jax.ShapeDtypeStruct(...  77.8 us
    unnamed x2, local copies, waits for them, and re-layouts  3.98 us

profile of v2, /device:TPU:16, one launch (start us, length us, event | category | flops | bytes accessed | tf_op | source)
XLA Modules:
  0.0 82.5 jit_solution(13920041725794314912)
XLA Ops:
  0.6 77.8 %mgrit_cycle.1 = (f32[4,1,8,8,8,128]{5,4,3,2,1,0:T(8,128)}, f32[1,1,8,8,8,128]{5,4,3,2,1,0:T(8,128)}) custom-call(f32[8,8,8,128]{3,2,1,0:T(8,128)} %bitcast.4, f32[4,1,8,8,8,128]{5,4,3,2,1,0:T(8,128)} %refs_1_.1, bf16[4,3,1152,128]{3,2,1,0:T(8,128)(2,1)} %bitcast.3, f32[4,1,1,128]{3,2,1,0:T(1,128)} %bitcast.5), custom_call_target="tpu_custom_call" | custom-call | tf_op jit(solution)/shard_map/mgrit_cycle/pallas_call | solution.py:342
  78.5 2.3 %copy.8 = f32[4,1,8,8,8,128]{5,4,3,2,1,0:T(8,128)} copy(f32[4,1,8,8,8,128]{5,4,3,2,1,0:T(8,128)} %get-tuple-element.4) | data formatting | bytes 2097152
  80.8 1.7 %copy.9 = f32[1,1,8,8,8,128]{5,4,3,2,1,0:T(8,128)} copy(f32[1,1,8,8,8,128]{5,4,3,2,1,0:T(8,128)} %get-tuple-element.5) | data formatting | bytes 524288

commit v3 on v2

--- a/solution.py
+++ b/solution.py
@@ -230,9 +230,12 @@
         @pl.when(takes(rel))
         def _(rel=rel):
             sib_copy(rel, 1 - core).wait_recv()
+
+        @pl.when(jnp.logical_and(takes(rel), pos < span_low))
+        def _(rel=rel):
             g_arrival(rel).wait_recv()
 
-    def chain(count):
+    def chain(count, arriving=False):
         def step(turn, carry):
             state = cur[...]
             mixed = mix(state, lead_w.at[turn])
@@ -242,6 +245,9 @@
                 head[...] = state
                 head_mix[...] = mixed
 
+            if arriving:
+                rel = lax.rem(pos + COARSEN - turn, COARSEN)
+                pl.when(rel > 0)(g_arrival(rel).wait_recv)
             after = state + coarse_size * mixed + defects[turn]
             cur[...] = after
             return carry
@@ -262,7 +268,7 @@
     @pl.when(is_upper)
     def _():
         cur[...] = jnp.where(group_in_first, inputs_ref[...], group_in[...])
-        chain(COARSEN)
+        chain(COARSEN, arriving=True)
         corner_out[...] = cur[...]
         pl.when(upper_sends)(relaxed.start)
         pl.when(follows)(relaxed.wait_recv)

time: 82.6 us -> 79.1 us (0.958)
  Pallas kernels: 77.8 us -> 74.3 us
    pallas_call x1, Pallas kernels: 77.8 us -> 74.3 us  [shards(): pl.pallas_call(body, name='mgrit_cycle', out_shape=(jax.ShapeDtypeStruct(...]
where the time goes in v3:
time: 79.1 us; the launch traced here: 78.9 us
  Pallas kernels  74.3 us (94%)
  local copies, waits for them, and re-layouts  3.98 us (5%)
    pallas_call x1, Pallas kernels, shards(): pl.pallas_call(body, name='mgrit_cycle', out_shape=(jax.ShapeDtypeStruct(...  74.3 us
    unnamed x2, local copies, waits for them, and re-layouts  3.98 us

profile of v3, /device:TPU:16, one launch (start us, length us, event | category | flops | bytes accessed | tf_op | source)
XLA Modules:
  0.0 78.9 jit_solution(3423289746186189739)
XLA Ops:
  0.6 74.3 %mgrit_cycle.1 = (f32[4,1,8,8,8,128]{5,4,3,2,1,0:T(8,128)}, f32[1,1,8,8,8,128]{5,4,3,2,1,0:T(8,128)}) custom-call(f32[8,8,8,128]{3,2,1,0:T(8,128)} %bitcast.4, f32[4,1,8,8,8,128]{5,4,3,2,1,0:T(8,128)} %refs_1_.1, bf16[4,3,1152,128]{3,2,1,0:T(8,128)(2,1)} %bitcast.3, f32[4,1,1,128]{3,2,1,0:T(1,128)} %bitcast.5), custom_call_target="tpu_custom_call" | custom-call | tf_op jit(solution)/shard_map/mgrit_cycle/pallas_call | solution.py:348
  75.0 2.3 %copy.8 = f32[4,1,8,8,8,128]{5,4,3,2,1,0:T(8,128)} copy(f32[4,1,8,8,8,128]{5,4,3,2,1,0:T(8,128)} %get-tuple-element.4) | data formatting | bytes 2097152
  77.3 1.7 %copy.9 = f32[1,1,8,8,8,128]{5,4,3,2,1,0:T(8,128)} copy(f32[1,1,8,8,8,128]{5,4,3,2,1,0:T(8,128)} %get-tuple-element.5) | data formatting | bytes 524288
